TPU v7x, 256 devices: a whole 4x4x8 slice. The times are simulated.
256 devices in a mesh: grp: 16 (over y_hi, x, core), pose: 16 (over y_lo, z).
Axes of the slice: x: 4, y: 4 (y_hi: 2, y_lo: 2; y = y_hi * 2 + y_lo), z: 8, core: 2. Of those that a mesh axis runs over, the one named last changes fastest.
Arguments:
- particles: bfloat16 [81920, 16384], P(('grp', 'pose')), may hold values from -64 to 64
- projections: bfloat16 [128, 16384], P('pose'), may hold values from -1.5 to 1.5
- ctf_table: bfloat16 [32, 16384], replicated, may hold values from 0.099609375 to 1
- group_ids: int32 [81920], P(('grp', 'pose')), may hold values from 0 to 31
Outputs:
- gradient: float32 [128, 16384], P('pose', 'grp')
- log_norm: float32 [81920], P(('grp', 'pose'))
All inputs are finite; a program needn't handle non-finite values.
Results may differ from a plain program's by a relative error of at most 0.0065.
Values may be sent and summed in bfloat16 or wider, within the bound.
No kernel may reach another device: no remote copies, remote signals or barrier semaphores. Data moves between devices by JAX's collectives and lax.ppermute only.
A program may use at most 128 MiB of HBM per device.

v0:
```python
import math
import jax
import jax.numpy as jnp
from jax import lax
from jax.sharding import PartitionSpec as P


def shards(particles, projections, ctf_table, group_ids):
    high = lax.Precision.HIGHEST
    part_count = particles.shape[0]
    feature_count = particles.shape[1]
    group_count = ctf_table.shape[0]
    pose_local = projections.shape[0]
    pose_total = pose_local * lax.axis_size("pose")
    particle_total = part_count * lax.axis_size("grp") * lax.axis_size("pose")
    inverse = 4.0 / math.sqrt(feature_count)
    factor = pose_total / particle_total
    one_hot = (group_ids[:, None] == jnp.arange(group_count, dtype=jnp.int32)[None, :]).astype(
        jnp.bfloat16
    )
    one_hot_f32 = one_hot.astype(jnp.float32)
    ctf_rows = jnp.dot(one_hot, ctf_table, preferred_element_type=jnp.bfloat16)
    weighted = ctf_rows * particles
    ctf_square = jnp.square(ctf_table.astype(jnp.float32))
    gathered = lax.all_gather(projections, "pose", axis=0, tiled=True)
    raw_dots = lax.dot_general(
        weighted, gathered, (((1,), (1,)), ((), ())), preferred_element_type=jnp.float32
    )
    model_f32 = gathered.astype(jnp.float32)
    norms = lax.dot_general(
        ctf_square,
        model_f32 * model_f32,
        (((1,), (1,)), ((), ())),
        precision=high,
        preferred_element_type=jnp.float32,
    )
    picked = jnp.dot(one_hot_f32, norms, precision=high)
    scores = inverse * (raw_dots - 0.5 * picked)
    row_peak = jnp.max(scores, axis=1, keepdims=True)
    log_norm = row_peak[:, 0] + jnp.log(jnp.sum(jnp.exp(scores - row_peak), axis=1))
    weights = jnp.exp(scores - log_norm[:, None]).astype(jnp.bfloat16)
    pose_mass = lax.dot_general(
        weights, one_hot, (((0,), (0,)), ((), ())), preferred_element_type=jnp.float32
    )
    numerator = lax.dot_general(
        weights, weighted, (((0,), (0,)), ((), ())), preferred_element_type=jnp.float32
    )
    model_rows = gathered.astype(jnp.float32)
    numerator = numerator - model_rows * jnp.dot(pose_mass, ctf_square, precision=high)
    pose_share = lax.psum_scatter(factor * numerator, "pose", scatter_dimension=0, tiled=True)
    out_block = lax.psum_scatter(pose_share, "grp", scatter_dimension=1, tiled=True)
    return (out_block, log_norm)


def solution(mesh):
    return jax.shard_map(
        shards,
        mesh=mesh,
        in_specs=(P(("grp", "pose"), None), P("pose", None), P(), P(("grp", "pose"))),
        out_specs=(P("pose", "grp"), P(("grp", "pose"))),
        check_vma=False,
    )
```

profile of v0, /device:TPU:2, one launch (start us, length us, event | category | flops | bytes accessed | tf_op | source)
XLA Modules:
  0.0 300.7 jit_solution(8398676469700784404)
XLA Ops:
  7.2 0.0 all-gather.2.cloned.1.call-start
  7.2 0.7 all-gather.2.cloned.1.call-update
  7.9 0.0 copy-start.1
  7.9 0.0 reduce-scatter.3.cloned.1.call-start
  8.0 9.7 %convolution_multiply_fusion.1 = bf16[320,16384]{1,0:T(8,128)(2,1)} fusion(bf16[320,16384]{1,0:T(8,128)(2,1)} %param.4, bf16[32,16384]{1,0:T(8,128)(2,1)} %param.6, s32[320]{0:T(512)} %param.7), kind=kOutput, calls=%fused_computation.3 | convolution fusion | flops 340797440 | bytes 22021376 | tf_op jit(solution)/shard_map/dot_general | solution.py:22
  17.7 72.0 %all-gather.2.cloned.1.call-done = bf16[128,16384]{1,0:T(8,128)(2,1)} async-done(((bf16[8,16384]{1,0:T(8,128)(2,1)}), bf16[128,16384]{1,0:T(8,128)(2,1)}) %all-gather.2.cloned.1.call-update) | async-done | bytes 4194320 | tf_op jit(solution)/shard_map/all_gather | solution.py:25
  89.6 0.0 copy-done.1
  89.6 10.0 %fusion.2 = f32[32,128]{1,0:T(8,128)S(1)} fusion(bf16[128,16384]{1,0:T(8,128)(2,1)} %all-gather.2.cloned.1.call-done, bf16[32,16384]{1,0:T(8,128)(2,1)S(1)} %copy-done.1), kind=kOutput, calls=%fused_computation.5 | convolution fusion | flops 810549248 | bytes 5259264 | tf_op jit(solution)/shard_map/dot_general | solution.py:30
  99.6 0.0 copy-start.2
  99.6 0.0 slice-start.1
  99.6 0.0 slice-start.2
  99.7 7.0 %fusion.11 = f32[320,128]{1,0:T(8,128)S(1)} fusion(bf16[320,16384]{1,0:T(8,128)(2,1)} %convolution_multiply_fusion.1, bf16[128,16384]{1,0:T(8,128)(2,1)} %all-gather.2.cloned.1.call-done), kind=kOutput, calls=%fused_computation.20 | convolution fusion | flops 1342177280 | bytes 14843904 | tf_op jit(solution)/shard_map/dot_general | solution.py:26
  106.6 0.0 copy-done.2
  106.6 0.4 fusion.10
  107.0 0.2 exponential_reduce_fusion
  107.3 0.0 copy-start.3
  107.3 2.5 fusion.9
  109.8 0.3 fusion.5
  110.1 10.2 %fusion.1 = f32[128,16384]{1,0:T(8,128)} fusion(f32[128,16384]{1,0:T(8,128)S(1)} %fusion.9, f32[128,32]{1,0:T(8,128)S(1)} %fusion.5, bf16[128,16384]{1,0:T(8,128)(2,1)S(1)} %copy-done, bf16[32,16384]{1,0:T(8,128)(2,1)S(1)} %copy-done.1), kind=kOutput, calls=%fused_computation.2 | convolution fusion | flops 814743552 | bytes 22036480 | tf_op jit(solution)/shard_map/dot_general | solution.py:49
  120.4 0.0 reduce-scatter.3.cloned.1.call-update
  120.4 0.0 reduce-scatter.5.cloned.1.call-start
  120.4 98.7 %reduce-scatter.3.cloned.1.call-done = f32[8,16384]{1,0:T(8,128)} async-done(((f32[128,16384]{1,0:T(8,128)}), f32[8,16384]{1,0:T(8,128)}) %reduce-scatter.3.cloned.1.call-update) | async-done | bytes 524304 | tf_op jit(solution)/shard_map/reduce_scatter | solution.py:50
  219.1 0.0 reduce-scatter.5.cloned.1.call-update
  219.1 75.0 %reduce-scatter.5.cloned.1.call-done = f32[8,1024]{1,0:T(8,128)} async-done(((f32[8,16384]{1,0:T(8,128)}), f32[8,1024]{1,0:T(8,128)}) %reduce-scatter.5.cloned.1.call-update) | async-done | bytes 32784 | tf_op jit(solution)/shard_map/reduce_scatter | solution.py:51
  (9 shorter events, 0.0 us)
Async XLA Ops:
  7.2 82.5 %all-gather.2.cloned.1.call-start = ((), (), s32[]{:S(2)}) async-start(), calls=%async_computation.2 | async-start | bytes 4456448 | tf_op jit(solution)/shard_map/all_gather | solution.py:25
  7.9 81.7 %copy-start.1 = (bf16[32,16384]{1,0:T(8,128)(2,1)S(1)}, bf16[32,16384]{1,0:T(8,128)(2,1)}, u32[]{:S(2)}) copy-start(bf16[32,16384]{1,0:T(8,128)(2,1)} %param.6) | copy-start | bytes 3145732
  7.9 211.2 %reduce-scatter.3.cloned.1.call-start = ((), (), s32[]{:S(2)}) async-start(), calls=%async_computation.3 | async-start | bytes 8912896 | tf_op jit(solution)/shard_map/reduce_scatter | solution.py:50
  89.6 17.6 %slice-start = ((s8[10485760]{0:T(1024)(128)(4,1)}), s8[4194304]{0:T(1024)(128)(4,1)S(1)}, s32[]{:S(2)}) async-start(s8[10485760]{0:T(1024)(128)(4,1)} %bitcast.6), calls=%async_computation.5 | async-start | bytes 8388608
  99.6 7.0 %copy-start.2 = (s32[320]{0:T(512)S(1)}, s32[320]{0:T(512)}, u32[]{:S(2)}) copy-start(s32[320]{0:T(512)} %param.7) | copy-start | bytes 3844
  99.6 7.6 %slice-start.1 = ((s8[10485760]{0:T(1024)(128)(4,1)}), s8[4194304]{0:T(1024)(128)(4,1)S(1)}, s32[]{:S(2)}) async-start(s8[10485760]{0:T(1024)(128)(4,1)} %bitcast.6), calls=%async_computation.6 | async-start | bytes 8388608
  99.6 7.6 %slice-start.2 = ((s8[10485760]{0:T(1024)(128)(4,1)}), s8[2097152]{0:T(1024)(128)(4,1)S(1)}, s32[]{:S(2)}) async-start(s8[10485760]{0:T(1024)(128)(4,1)} %bitcast.6), calls=%async_computation.7 | async-start | bytes 4194304
  107.3 2.5 copy-start.3
  107.3 2.8 copy-start
  120.4 173.8 %reduce-scatter.5.cloned.1.call-start = ((), (), s32[]{:S(2)}) async-start(), calls=%async_computation.4 | async-start | bytes 557056 | tf_op jit(solution)/shard_map/reduce_scatter | solution.py:51
Sparse Core Ops, SparseCore 0:
  9.8 79.7 all-gather.1
  120.5 98.5 reduce-scatter.2
  223.8 70.3 reduce-scatter.4
where the time goes:
time: 301 us
  waiting for transfers between devices  246 us (82%)
  matrix products  40 us (13%)
  between operations  13.9 us (5%)
    reduce_scatter x1, waiting for transfers between devices, shards(): lax.psum_scatter(factor * numerator, 'pose', scatter_dimension=0, tiled=T...  98.7 us
    reduce_scatter x1, waiting for transfers between devices, shards(): lax.psum_scatter(pose_share, 'grp', scatter_dimension=1, tiled=True)  75 us
    all_gather x1, waiting for transfers between devices, shards(): gathered = lax.all_gather(projections, 'pose', axis=0, tiled=True)  72 us
    dot_general x1, matrix products, shards(): jnp.dot(pose_mass, ctf_square, precision=high)  10.2 us
    dot_general x1, matrix products, shards(): lax.dot_general(ctf_square, model_f32 * model_f32, (((1,), (1,)), ((), ()...  9.99 us
    dot_general x1, matrix products, shards(): ctf_rows = jnp.dot(one_hot, ctf_table, preferred_element_type=jnp.bfloat16)  9.71 us
    dot_general x1, matrix products, shards(): lax.dot_general(weighted, gathered, (((1,), (1,)), ((), ())), preferred_e...  6.95 us
  transfers between devices with their start and end apart: 3, of which 3 were waited for; matrix products, arithmetic and copies ran while one was open for 3% of the time, Pallas kernels for 0%

commit v1 on v0

--- a/solution.py
+++ b/solution.py
@@ -22,7 +22,9 @@
     ctf_rows = jnp.dot(one_hot, ctf_table, preferred_element_type=jnp.bfloat16)
     weighted = ctf_rows * particles
     ctf_square = jnp.square(ctf_table.astype(jnp.float32))
-    gathered = lax.all_gather(projections, "pose", axis=0, tiled=True)
+    gathered = jnp.concatenate(
+        lax.all_to_all(jnp.stack([projections] * lax.axis_size("pose")), "pose", 0, 0), axis=0
+    )
     raw_dots = lax.dot_general(
         weighted, gathered, (((1,), (1,)), ((), ())), preferred_element_type=jnp.float32
     )

time: 301 us -> 332 us (1.10)
  waiting for transfers between devices: 246 us -> 265 us
  starting transfers between devices: 0.12 us -> 9.72 us
  local copies, waits for them, and re-layouts: 0.03 us -> 3.45 us
    all_to_all x0 -> x1, waiting for transfers between devices: none -> 87.1 us  [shards(): lax.all_to_all(jnp.stack([projections] * lax.axis_size('pose')), 'pose',...]
    all_gather x1 -> x0, waiting for transfers between devices: 72 us -> none  [shards(): gathered = lax.all_gather(projections, 'pose', axis=0, tiled=True)]
    all_to_all x0 -> x1, starting transfers between devices: none -> 9.63 us  [shards(): lax.all_to_all(jnp.stack([projections] * lax.axis_size('pose')), 'pose',...]
    reduce_scatter x1, waiting for transfers between devices: 98.7 us -> 103 us  [shards(): lax.psum_scatter(factor * numerator, 'pose', scatter_dimension=0, tiled=T...]
    another operation x0 -> x1, local copies, waits for them, and re-layouts: none -> 3.42 us  [shards(): jnp.stack([projections] * lax.axis_size('pose'))]
  transfers between devices with their start and end apart: 3 -> 3, of which waited for: 3 -> 3; matrix products, arithmetic and copies ran while one was open for 3% -> 2% of each run, Pallas kernels for 0% -> 0%
where the time goes in v1:
time: 332 us
  waiting for transfers between devices  265 us (80%)
  matrix products  39.8 us (12%)
  between operations  14.2 us (4%)
  starting transfers between devices  9.72 us (3%)
  local copies, waits for them, and re-layouts  3.45 us (1%)
    reduce_scatter x1, waiting for transfers between devices, shards(): lax.psum_scatter(factor * numerator, 'pose', scatter_dimension=0, tiled=T...  103 us
    all_to_all x1, waiting for transfers between devices, shards(): lax.all_to_all(jnp.stack([projections] * lax.axis_size('pose')), 'pose',...  87.1 us
    reduce_scatter x1, waiting for transfers between devices, shards(): lax.psum_scatter(pose_share, 'grp', scatter_dimension=1, tiled=True)  75 us
    dot_general x1, matrix products, shards(): jnp.dot(pose_mass, ctf_square, precision=high)  11.7 us
    dot_general x1, matrix products, shards(): lax.dot_general(ctf_square, model_f32 * model_f32, (((1,), (1,)), ((), ()...  10 us
    all_to_all x1, starting transfers between devices, shards(): lax.all_to_all(jnp.stack([projections] * lax.axis_size('pose')), 'pose',...  9.63 us
    dot_general x1, matrix products, shards(): ctf_rows = jnp.dot(one_hot, ctf_table, preferred_element_type=jnp.bfloat16)  8.04 us
    dot_general x1, matrix products, shards(): lax.dot_general(weighted, gathered, (((1,), (1,)), ((), ())), preferred_e...  6.96 us
  transfers between devices with their start and end apart: 3, of which 3 were waited for; matrix products, arithmetic and copies ran while one was open for 2% of the time, Pallas kernels for 0%

profile of v1, /device:TPU:2, one launch (start us, length us, event | category | flops | bytes accessed | tf_op | source)
XLA Modules:
  0.0 332.2 jit_solution(8731149569727703902)
XLA Ops:
  7.2 3.4 %stack.2 = bf16[16,8,16384]{2,1,0:T(8,128)(2,1)} broadcast(bf16[8,16384]{1,0:T(8,128)(2,1)} %param.5), dimensions={1,2} | broadcast | bytes 4456448 | tf_op jit(solution)/shard_map/stack | solution.py:26
  10.6 9.6 %all-to-all-start = ((bf16[16,8,16384]{2,1,0:T(8,128)(2,1)}), bf16[16,8,16384]{2,1,0:T(8,128)(2,1)}, u32[]{:S(2)}, u32[]{:S(2)}) async-start(bf16[16,8,16384]{2,1,0:T(8,128)(2,1)} %stack.2), calls=%async_computation | async-start | bytes 8388608 | tf_op jit(solution)/shard_map/all_to_all | solution.py:26
  20.2 0.0 reduce-scatter.3.cloned.1.call-start
  20.3 0.0 copy-done.1
  20.3 0.0 copy-done
  20.3 8.0 %convolution_multiply_fusion.1 = bf16[320,16384]{1,0:T(8,128)(2,1)} fusion(bf16[320,16384]{1,0:T(8,128)(2,1)} %param.4, bf16[32,16384]{1,0:T(8,128)(2,1)S(1)} %copy-done, s32[320]{0:T(512)S(1)} %copy-done.1), kind=kOutput, calls=%fused_computation.3 | convolution fusion | flops 340797440 | bytes 22021376 | tf_op jit(solution)/shard_map/dot_general | solution.py:22
  28.4 87.1 %all-to-all-done = bf16[16,8,16384]{2,1,0:T(8,128)(2,1)} async-done(((bf16[16,8,16384]{2,1,0:T(8,128)(2,1)}), bf16[16,8,16384]{2,1,0:T(8,128)(2,1)}, u32[]{:S(2)}, u32[]{:S(2)}) %all-to-all-start) | async-done | bytes 4194336 | tf_op jit(solution)/shard_map/all_to_all | solution.py:26
  115.5 10.0 %fusion.2 = f32[32,128]{1,0:T(8,128)S(1)} fusion(bf16[16,8,16384]{2,1,0:T(8,128)(2,1)} %all-to-all-done, bf16[32,16384]{1,0:T(8,128)(2,1)S(1)} %copy-done), kind=kOutput, calls=%fused_computation.5 | convolution fusion | flops 810549248 | bytes 5259264 | tf_op jit(solution)/shard_map/dot_general | solution.py:32
  125.5 0.0 slice-start.1
  125.5 0.0 slice-start.2
  125.5 7.0 %fusion.4 = f32[320,128]{1,0:T(8,128)S(1)} fusion(bf16[320,16384]{1,0:T(8,128)(2,1)} %convolution_multiply_fusion.1, bf16[16,8,16384]{2,1,0:T(8,128)(2,1)} %all-to-all-done), kind=kOutput, calls=%fused_computation.7 | convolution fusion | flops 1342177280 | bytes 14843904 | tf_op jit(solution)/shard_map/dot_general | solution.py:28
  132.4 0.4 fusion.13
  132.8 0.2 exponential_reduce_fusion
  133.1 0.0 slice-done
  133.1 0.0 slice-done.1
  133.1 0.0 copy-start.2
  133.1 2.5 fusion.12
  135.6 0.3 fusion.8
  135.9 11.7 %fusion.1 = f32[128,16384]{1,0:T(8,128)} fusion(f32[128,16384]{1,0:T(8,128)S(1)} %fusion.12, f32[128,32]{1,0:T(8,128)S(1)} %fusion.8, bf16[16,8,16384]{2,1,0:T(8,128)(2,1)} %all-to-all-done, bf16[32,16384]{1,0:T(8,128)(2,1)S(1)} %copy-done), kind=kOutput, calls=%fused_computation.2 | convolution fusion | flops 814743552 | bytes 22036480 | tf_op jit(solution)/shard_map/dot_general | solution.py:51
  147.6 0.0 reduce-scatter.3.cloned.1.call-update
  147.6 0.0 reduce-scatter.5.cloned.1.call-start
  147.7 102.6 %reduce-scatter.3.cloned.1.call-done = f32[8,16384]{1,0:T(8,128)} async-done(((f32[128,16384]{1,0:T(8,128)}), f32[8,16384]{1,0:T(8,128)}) %reduce-scatter.3.cloned.1.call-update) | async-done | bytes 524304 | tf_op jit(solution)/shard_map/reduce_scatter | solution.py:52
  250.3 0.0 reduce-scatter.5.cloned.1.call-update
  250.3 75.0 %reduce-scatter.5.cloned.1.call-done = f32[8,1024]{1,0:T(8,128)} async-done(((f32[8,16384]{1,0:T(8,128)}), f32[8,1024]{1,0:T(8,128)}) %reduce-scatter.5.cloned.1.call-update) | async-done | bytes 32784 | tf_op jit(solution)/shard_map/reduce_scatter | solution.py:53
  (7 shorter events, 0.0 us)
Async XLA Ops:
  7.2 13.1 %copy-start.1 = (s32[320]{0:T(512)S(1)}, s32[320]{0:T(512)}, u32[]{:S(2)}) copy-start(s32[320]{0:T(512)} %param.7) | copy-start | bytes 3844
  7.2 13.1 %copy-start = (bf16[32,16384]{1,0:T(8,128)(2,1)S(1)}, bf16[32,16384]{1,0:T(8,128)(2,1)}, u32[]{:S(2)}) copy-start(bf16[32,16384]{1,0:T(8,128)(2,1)} %param.6) | copy-start | bytes 3145732
  10.6 104.8 %all-to-all-start = ((bf16[16,8,16384]{2,1,0:T(8,128)(2,1)}), bf16[16,8,16384]{2,1,0:T(8,128)(2,1)}, u32[]{:S(2)}, u32[]{:S(2)}) async-start(bf16[16,8,16384]{2,1,0:T(8,128)(2,1)} %stack.2), calls=%async_computation | async-start | bytes 8388608 | tf_op jit(solution)/shard_map/all_to_all | solution.py:26
  20.2 230.0 %reduce-scatter.3.cloned.1.call-start = ((), (), s32[]{:S(2)}) async-start(), calls=%async_computation.3 | async-start | bytes 8912896 | tf_op jit(solution)/shard_map/reduce_scatter | solution.py:52
  115.5 17.6 %slice-start = ((s8[10485760]{0:T(1024)(128)(4,1)}), s8[4194304]{0:T(1024)(128)(4,1)S(1)}, s32[]{:S(2)}) async-start(s8[10485760]{0:T(1024)(128)(4,1)} %bitcast.13), calls=%async_computation.5 | async-start | bytes 8388608
  125.5 7.6 %slice-start.1 = ((s8[10485760]{0:T(1024)(128)(4,1)}), s8[4194304]{0:T(1024)(128)(4,1)S(1)}, s32[]{:S(2)}) async-start(s8[10485760]{0:T(1024)(128)(4,1)} %bitcast.13), calls=%async_computation.6 | async-start | bytes 8388608
  125.5 7.6 %slice-start.2 = ((s8[10485760]{0:T(1024)(128)(4,1)}), s8[2097152]{0:T(1024)(128)(4,1)S(1)}, s32[]{:S(2)}) async-start(s8[10485760]{0:T(1024)(128)(4,1)} %bitcast.13), calls=%async_computation.7 | async-start | bytes 4194304
  133.1 2.5 copy-start.2
  147.6 177.7 %reduce-scatter.5.cloned.1.call-start = ((), (), s32[]{:S(2)}) async-start(), calls=%async_computation.4 | async-start | bytes 557056 | tf_op jit(solution)/shard_map/reduce_scatter | solution.py:53
Sparse Core Ops, SparseCore 0:
  147.8 102.4 reduce-scatter.2
  254.9 70.3 reduce-scatter.4
